TPU v7x, 32 devices: a whole 2x2x4 slice. The times are simulated.
32 devices in a mesh: groups: 2 (over x), cache: 16 (over z, y, core).
Axes of the slice: x: 2, y: 2, z: 4, core: 2. Of those that a mesh axis runs over, the one named last changes fastest.
Arguments:
- prefix_len: int32 [32], P('groups'), parts along dimension 0, may hold values from 128 to 1024, as said below
- hits: int32 [32, 1], P('groups'), parts along dimension 0, may hold values from 0 to 15, as said below
- span_block: int32 [32, 16], P('groups'), parts along dimension 0, may hold values from 0 to 15, each once within a row
- queries: bfloat16 [2048, 2048], P(('groups', 'cache')), parts along dimension 0, may hold values from -100 to 100
- fresh_keys: bfloat16 [2048, 128], P(('groups', 'cache')), parts along dimension 0, may hold values from -4 to 4
- fresh_values: bfloat16 [2048, 128], P(('groups', 'cache')), parts along dimension 0, may hold values from -4 to 4
- cache_keys: bfloat16 [65536, 128], P(('groups', 'cache')), parts along dimension 0, may hold values from -4 to 4
- cache_values: bfloat16 [65536, 128], P(('groups', 'cache')), parts along dimension 0, may hold values from -4 to 4
Outputs:
- attended: bfloat16 [2048, 2048], P(('groups', 'cache')), parts along dimension 0
There are 2 independent parts, one for each index of `groups`. A program takes and returns all parts, laid end to end along the dimension named above; each array names one. Nothing has to cross between parts.
Inputs may be any that keep to these rules, and one draw needn't show every extreme that they name: `prefix_len`: every request's prefix holds at least 128 tokens, and one request in every draw holds exactly 1024. `hits`: each row names 1 different devices. Each device is named by at most 2 requests; 4 devices are named by exactly 2, half of them by one, a quarter by none. `span_block`: each row is a permutation.
All inputs are finite; a program needn't handle non-finite values.
Results may differ from a plain program's by a relative error of at most 0.0065.
Values may be sent and summed in bfloat16 or wider, within the bound.
A program may use at most 64 MiB of HBM per device.

v0:
```python
import math
import jax
import jax.numpy as jnp
from jax import lax
from jax.sharding import PartitionSpec as P

HEADS = 16
HD = 128
PAGE = 128
CAP = 2
REQUESTS = 16
TOK_REQ = 4
PAGES_DEV = 16
floor_score = -1e30


def owner_block(query_block, page_keys, page_values, visible):
    scale = HD ** (-0.5)
    scores = (
        jnp.einsum("thd,kd->thk", query_block, page_keys, preferred_element_type=jnp.float32)
        * scale
    )
    scores = jnp.where(visible, scores, floor_score)
    maxima = jnp.max(scores, axis=2)
    weights = jnp.exp(scores - maxima[:, :, None]) * visible
    totals = jnp.maximum(jnp.sum(weights, axis=2), 1.0)
    summed = jnp.einsum(
        "thk,kd->thd", weights.astype(jnp.bfloat16), page_values, preferred_element_type=jnp.float32
    )
    partial_out = (summed / totals[:, :, None]).astype(jnp.bfloat16)
    return (partial_out, maxima + jnp.log(totals))


def serve_slots(slot_queries, slot_keys, slot_values, slot_visible, devices):
    per_group = math.gcd(devices, 16)

    def one_slot(packed):
        queries_in, page_keys, page_values, visible = packed
        grouped = queries_in.reshape(devices // per_group, per_group * TOK_REQ, HEADS, HD)

        def one_group(query_block):
            return owner_block(query_block, page_keys, page_values, visible)

        outputs, lse_rows = lax.map(one_group, grouped)
        return (
            outputs.reshape(devices, TOK_REQ, HEADS * HD),
            lse_rows.reshape(devices, TOK_REQ, HEADS),
        )

    return lax.map(one_slot, (slot_queries, slot_keys, slot_values, slot_visible))


def body(prefix_len, hits, span_block, queries, fresh_keys, fresh_values, cache_keys, cache_values):
    devices = lax.axis_size("cache")
    myself = lax.axis_index("cache")
    hit_count = hits.shape[1]
    region = PAGES_DEV // CAP * PAGE
    per_device = REQUESTS * TOK_REQ
    scale = HD ** (-0.5)
    offsets = jnp.arange(TOK_REQ, dtype=jnp.int32)
    request_ids = jnp.arange(REQUESTS, dtype=jnp.int32)
    owner_ids = jnp.arange(devices, dtype=jnp.int32)
    slot_ids = jnp.arange(CAP, dtype=jnp.int32)
    is_named = jnp.any(hits[:, :, None] == owner_ids[None, None, :], axis=1).astype(jnp.int32)
    earlier = (request_ids[None, :] < request_ids[:, None]).astype(jnp.int32)
    slot_rank = jnp.sum(earlier[:, :, None] * is_named[None, :, :], axis=1)
    holding = (is_named[None] == 1) & (slot_rank[None] == slot_ids[:, None, None])
    occupied = jnp.any(holding, axis=1)
    send_request = jnp.sum(holding * request_ids[None, :, None], axis=1)
    local_request = jnp.take(send_request, myself, axis=1)
    local_occupied = jnp.take(occupied, myself, axis=1)
    local_hits = jnp.take(hits, local_request, axis=0)
    hit_place = jnp.sum(
        jnp.where(local_hits == myself, jnp.arange(hit_count, dtype=jnp.int32)[None, :], 0), axis=1
    )
    page_limit = jnp.take(prefix_len, local_request)
    prefix_spot = hit_place[:, None] * region + jnp.arange(region, dtype=jnp.int32)[None, :]
    slot_visible = local_occupied[:, None] & (prefix_spot < page_limit[:, None])
    region_keys = cache_keys.reshape(CAP, region, HD)
    region_values = cache_values.reshape(CAP, region, HD)
    query_heads = queries.reshape(REQUESTS, TOK_REQ, HEADS, HD)
    my_blocks = jnp.take(span_block, myself, axis=1)
    query_spot = my_blocks[:, None] * TOK_REQ + offsets[None, :]
    running = jnp.full((REQUESTS, TOK_REQ, HEADS), floor_score, jnp.float32)
    key_piece = lax.all_gather(fresh_keys, "cache", axis=0, tiled=True)
    value_piece = lax.all_gather(fresh_values, "cache", axis=0, tiled=True)
    count = key_piece.shape[0] // per_device
    key_rows = jnp.transpose(key_piece.reshape(count, REQUESTS, TOK_REQ, HD), (1, 0, 2, 3)).reshape(
        REQUESTS, count * TOK_REQ, HD
    )
    value_rows = jnp.transpose(
        value_piece.reshape(count, REQUESTS, TOK_REQ, HD), (1, 0, 2, 3)
    ).reshape(REQUESTS, count * TOK_REQ, HD)
    key_spot = (span_block[:, :, None] * TOK_REQ + offsets[None, None, :]).reshape(
        REQUESTS, count * TOK_REQ
    )
    visible = (key_spot[:, None, :] <= query_spot[:, :, None])[:, :, None, :]
    scores = (
        jnp.einsum("rthd,rkd->rthk", query_heads, key_rows, preferred_element_type=jnp.float32)
        * scale
    )
    scores = jnp.where(visible, scores, floor_score)
    highest = jnp.maximum(running, jnp.max(scores, axis=3))
    weights = jnp.exp(scores - highest[..., None]) * visible
    totals = jnp.sum(weights, axis=3)
    value_wide = value_rows.astype(jnp.float32)
    summed = jnp.einsum("rthk,rkd->rthd", weights, value_wide, precision=lax.Precision.HIGHEST)
    running, totals, summed = (highest, totals, summed)
    prompt_out = summed / totals[..., None]
    prompt_lse = running + jnp.log(totals)
    units = queries.reshape(REQUESTS, TOK_REQ, HEADS * HD)
    outgoing = jnp.take(units, send_request, axis=0)
    arrived_queries = lax.all_to_all(outgoing, "cache", split_axis=1, concat_axis=1, tiled=True)
    partial_out, partial_lse = serve_slots(
        arrived_queries, region_keys, region_values, slot_visible, devices
    )
    returned_out, returned_lse = (
        lax.all_to_all(
            partial_out.astype(jnp.float32), "cache", split_axis=1, concat_axis=1, tiled=True
        ).astype(partial_out.dtype),
        lax.all_to_all(partial_lse, "cache", split_axis=1, concat_axis=1, tiled=True),
    )
    flat_out = returned_out.reshape(CAP * devices, TOK_REQ, HEADS, HD)
    flat_lse = returned_lse.reshape(CAP * devices, TOK_REQ, HEADS)
    hit_rank = jnp.take_along_axis(slot_rank, hits, axis=1)
    source = hit_rank * devices + hits
    owner_out = jnp.take(flat_out, source, axis=0)
    owner_lse = jnp.take(flat_lse, source, axis=0)
    every_lse = jnp.concatenate([prompt_lse[:, None], owner_lse], axis=1)
    highest = jnp.max(every_lse, axis=1)
    shares = jnp.exp(every_lse - highest[:, None])
    combined = shares[:, 0, :, :, None] * prompt_out + jnp.einsum(
        "rith,rithd->rthd", shares[:, 1:], owner_out, preferred_element_type=jnp.float32
    )
    result = combined / jnp.sum(shares, axis=1)[..., None]
    return result.astype(jnp.bfloat16).reshape(per_device, HEADS * HD)


def solution(mesh):
    in_specs = (
        P("groups"),
        P("groups", None),
        P("groups", None),
        P(("groups", "cache"), None),
        P(("groups", "cache"), None),
        P(("groups", "cache"), None),
        P(("groups", "cache"), None),
        P(("groups", "cache"), None),
    )
    out_specs = P(("groups", "cache"), None)
    return jax.shard_map(body, mesh=mesh, in_specs=in_specs, out_specs=out_specs, check_vma=False)
```

profile of v0, /device:TPU:0, one launch (start us, length us, event | category | flops | bytes accessed | tf_op | source)
XLA Modules:
  0.0 96.3 jit_solution(12392458391359597815)
XLA Ops:
  0.0 0.8 broadcast_compare_fusion.1
  1.1 1.1 %reshape.331 = bf16[16,4,2048]{2,1,0:T(4,128)(2,1)S(1)} reshape(bf16[64,2048]{1,0:T(8,128)(2,1)} %param.13) | data formatting | bytes 524288 | tf_op jit(solution)/shard_map/reshape | solution.py:111
  2.1 1.0 %gather_fusion.1 = bf16[32,4,2048]{2,1,0:T(4,128)(2,1)S(1)} fusion(bf16[16,4,2048]{2,1,0:T(4,128)(2,1)S(1)} %reshape.331, s32[1024]{0:T(1024)S(1)} %pad_clamp_fusion.1), kind=kCustom, calls=%fused_computation.1 | custom fusion | bytes 1048704 | tf_op jit(solution)/shard_map/jit(_take)/gather | solution.py:112
  3.2 0.3 copy.71
  3.6 1.2 %copy.72 = bf16[2,16,4,2048]{3,2,0,1:T(4,128)(2,1)} copy(bf16[2,16,4,2048]{3,1,0,2:T(8,128)(2,1)S(1)} %broadcast_select_fusion) | data formatting | bytes 1048576 | tf_op jit(solution)/shard_map/jit(_take)/select_n | solution.py:112
  4.8 7.4 %all-to-all-start = ((bf16[2,16,4,2048]{3,2,0,1:T(4,128)(2,1)}), bf16[2,16,4,2048]{3,2,0,1:T(4,128)(2,1)S(1)}, u32[]{:S(2)}, u32[]{:S(2)}) async-start(bf16[2,16,4,2048]{3,2,0,1:T(4,128)(2,1)} %copy.72), calls=%async_computation | async-start | bytes 1048576 | tf_op jit(solution)/shard_map/all_to_all | solution.py:113
  12.5 0.2 select_reduce_fusion.1
  12.7 0.7 gather_fusion.4
  13.9 24.2 %all_gather.6 = bf16[1024,128]{1,0:T(8,128)(2,1)S(1)} all-gather(bf16[64,128]{1,0:T(8,128)(2,1)S(1)} %copy-done.4), channel_id=1, replica_groups=mesh['groups'=2,'cache'=16] {'cache'}, dimensions={0}, use_global_device_ids=true | all-gather | bytes 278528 | tf_op jit(solution)/shard_map/all_gather | solution.py:85
  38.3 0.6 gather_fusion
  39.0 0.4 fusion.43
  39.4 0.4 fusion.26
  40.0 7.6 %while.20 = (s32[]{:T(128)}, bf16[2,16,4,2048]{3,1,2,0:T(8,128)(2,1)S(1)}, f32[2,16,4,16]{3,2,0,1:T(4,128)S(1)}, pred[2,1024]{1,0:T(4,128)(4,1)S(1)}, bf16[2,16,...) while((s32[]{:T(128)}, ...), condition=%wide.region_8.9_spmd, body=%wide.region_5.0_spmd.sunk | while | flops 550765568 | bytes 15906925 | solution.py:50
  40.3 0.8 fusion.57
  41.1 1.2 %fusion.58 = f32[64,16]{1,0:T(8,128)S(1)} fusion(f32[64,16,1024]{2,1,0:T(8,128)S(1)} %get-tuple-element.216, f32[1024]{0:T(1024)S(1)} %convert_element_type.76, f32[64,16]{1,0:T(8,128)S(1)} %get-tuple-element.217, pred[1024]{0:T(1024)(128)(4,1)S(1)} %dynamic-slice_reduce_fusion.2), kind=kLoop, calls=%fused_computation.8.clone.1 | loop fusion | flops 5241856 | bytes 4207616 | tf_op jit(solution)/shard_map/while/body/eval_jaxpr/while/body/eval_jaxpr/reduce_sum | solution.py:26
  42.3 1.1 %fusion.59 = bf16[64,16,128]{2,1,0:T(8,128)(2,1)S(1)} fusion(f32[64,16,1024]{2,1,0:T(8,128)S(1)} %get-tuple-element.216, f32[1024]{0:T(1024)S(1)} %convert_element_type.76, f32[64,16]{1,0:T(8,128)S(1)} %get-tuple-element.217, pred[1024]{0:T(1024)(128)(4,1)S(1)} %dynamic-slice_reduce_fusion.2, f32[64,16]{1,0:T(8,128)S(1)} %get-tuple-element.218, ...), kind=kOutput, calls=%fused_computation.13.clone.1 | convolution fusion | flops 273940480 | bytes 4789252 | tf_op jit(solution)/shard_map/while/body/eval_jaxpr/while/body/eval_jaxpr/thk,kd->thd/dot_general | solution.py:27
  44.1 0.8 fusion.57
  44.9 1.2 %fusion.58 = f32[64,16]{1,0:T(8,128)S(1)} fusion(f32[64,16,1024]{2,1,0:T(8,128)S(1)} %get-tuple-element.216, f32[1024]{0:T(1024)S(1)} %convert_element_type.76, f32[64,16]{1,0:T(8,128)S(1)} %get-tuple-element.217, pred[1024]{0:T(1024)(128)(4,1)S(1)} %dynamic-slice_reduce_fusion.2), kind=kLoop, calls=%fused_computation.8.clone.1 | loop fusion | flops 5241856 | bytes 4207616 | tf_op jit(solution)/shard_map/while/body/eval_jaxpr/while/body/eval_jaxpr/reduce_sum | solution.py:26
  46.1 1.1 %fusion.59 = bf16[64,16,128]{2,1,0:T(8,128)(2,1)S(1)} fusion(f32[64,16,1024]{2,1,0:T(8,128)S(1)} %get-tuple-element.216, f32[1024]{0:T(1024)S(1)} %convert_element_type.76, f32[64,16]{1,0:T(8,128)S(1)} %get-tuple-element.217, pred[1024]{0:T(1024)(128)(4,1)S(1)} %dynamic-slice_reduce_fusion.2, f32[64,16]{1,0:T(8,128)S(1)} %get-tuple-element.218, ...), kind=kOutput, calls=%fused_computation.13.clone.1 | convolution fusion | flops 273940480 | bytes 4789252 | tf_op jit(solution)/shard_map/while/body/eval_jaxpr/while/body/eval_jaxpr/thk,kd->thd/dot_general | solution.py:27
  47.5 0.7 reshape.490
  48.3 3.5 %all-to-all-start.1 = ((f32[16,1,128]{2,1,0:T(1,128)}), f32[16,1,128]{2,1,0:T(1,128)S(1)}, u32[]{:S(2)}, u32[]{:S(2)}) async-start(f32[16,1,128]{2,1,0:T(1,128)} %reshape.490), calls=%async_computation.1 | async-start | bytes 16384 | tf_op jit(solution)/shard_map/all_to_all | solution.py:121
  51.7 22.4 %all_gather.7 = bf16[1024,128]{1,0:T(8,128)(2,1)S(1)} all-gather(bf16[64,128]{1,0:T(8,128)(2,1)S(1)} %copy-done.5), channel_id=1, replica_groups=mesh['groups'=2,'cache'=16] {'cache'}, dimensions={0}, use_global_device_ids=true | all-gather | bytes 278528 | tf_op jit(solution)/shard_map/all_gather | solution.py:86
  74.3 1.2 %copy.79 = bf16[2,16,4,2048]{3,2,0,1:T(4,128)(2,1)} copy(bf16[2,16,4,2048]{3,1,2,0:T(8,128)(2,1)S(1)} %get-tuple-element.65) | data formatting | bytes 1048576 | tf_op jit(solution)/shard_map/convert_element_type | solution.py:119
  75.5 3.6 %all-to-all-start.2 = ((bf16[2,16,4,2048]{3,2,0,1:T(4,128)(2,1)}), bf16[2,16,4,2048]{3,2,0,1:T(4,128)(2,1)S(1)}, u32[]{:S(2)}, u32[]{:S(2)}) async-start(bf16[2,16,4,2048]{3,2,0,1:T(4,128)(2,1)} %copy.79), calls=%async_computation.2 | async-start | bytes 1048576 | tf_op jit(solution)/shard_map/all_to_all | solution.py:118
  79.1 0.5 broadcast.506
  79.6 0.7 reduce.10
  80.4 0.6 gather_fusion.2
  81.2 12.3 %all-to-all-done.2 = bf16[2,16,4,2048]{3,2,0,1:T(4,128)(2,1)S(1)} async-done(((bf16[2,16,4,2048]{3,2,0,1:T(4,128)(2,1)}), bf16[2,16,4,2048]{3,2,0,1:T(4,128)(2,1)S(1)}, u32[]{:S(2)}, u32[]{:S(2)}) %all-to-all-start.2) | async-done | bytes 524320 | tf_op jit(solution)/shard_map/all_to_all | solution.py:118
  93.5 0.3 copy.80
  93.9 0.6 gather_fusion.3
  94.5 1.0 %fusion.25 = bf16[16,4,16,128]{3,2,1,0:T(8,128)(2,1)S(1)} fusion(bf16[16,64,128,1]{2,1,3,0:T(8,128)(2,1)S(1)} %bitcast.106, f32[16,4,16,64]{3,2,1,0:T(8,128)S(1)} %get-tuple-element.167, f32[16,4,16]{2,1,0:T(4,128)S(1)} %get-tuple-element.150, bf16[16,4,16,128]{3,2,1,0:T(8,128)(2,1)S(1)} %gather_fusion.3, f32[16,4,16]{2,1,0:T(4,128)S(1)} %get-tuple-element.161, ...), kind=kOutput, calls=%fused_computation.35 | convolution fusion | flops 101842944 | bytes 1085456 | tf_op jit(solution)/shard_map/rthk,rkd->rthd/dot_general | solution.py:107
  95.5 0.8 copy.98
  (77 shorter events, 3.3 us)
Async XLA Ops:
  0.0 38.2 %copy-start = (s32[16]{0:T(128)S(1)}, s32[16]{0:T(128)}, u32[]{:S(2)}) copy-start(s32[16]{0:T(128)} %param.10) | copy-start | bytes 196
  0.0 12.2 %copy-start.6 = (s32[16,1]{0,1:T(1,128)S(1)}, s32[16,1]{0,1:T(1,128)}, u32[]{:S(2)}) copy-start(s32[16,1]{0,1:T(1,128)} %param.11) | copy-start | bytes 196
  0.0 38.2 %copy-start.2 = (bf16[64,2048]{1,0:T(8,128)(2,1)S(1)}, bf16[64,2048]{1,0:T(8,128)(2,1)}, u32[]{:S(2)}) copy-start(bf16[64,2048]{1,0:T(8,128)(2,1)} %param.13) | copy-start | bytes 786436
  0.0 12.2 %copy-start.3 = (s32[16,16]{1,0:T(8,128)S(1)}, s32[16,16]{1,0:T(8,128)}, u32[]{:S(2)}) copy-start(s32[16,16]{1,0:T(8,128)} %param.12) | copy-start | bytes 3076
  0.0 13.9 %copy-start.4 = (bf16[64,128]{1,0:T(8,128)(2,1)S(1)}, bf16[64,128]{1,0:T(8,128)(2,1)}, u32[]{:S(2)}) copy-start(bf16[64,128]{1,0:T(8,128)(2,1)} %param.14) | copy-start | bytes 49156
  3.1 36.8 %copy-start.1 = (bf16[2048,128]{1,0:T(8,128)(2,1)S(1)}, bf16[2048,128]{1,0:T(8,128)(2,1)}, u32[]{:S(2)}) copy-start(bf16[2048,128]{1,0:T(8,128)(2,1)} %param.16) | copy-start | bytes 1572868
  3.1 36.8 %copy-start.7 = (bf16[2048,128]{1,0:T(8,128)(2,1)S(1)}, bf16[2048,128]{1,0:T(8,128)(2,1)}, u32[]{:S(2)}) copy-start(bf16[2048,128]{1,0:T(8,128)(2,1)} %param.17) | copy-start | bytes 1572868
  4.8 35.2 %all-to-all-start = ((bf16[2,16,4,2048]{3,2,0,1:T(4,128)(2,1)}), bf16[2,16,4,2048]{3,2,0,1:T(4,128)(2,1)S(1)}, u32[]{:S(2)}, u32[]{:S(2)}) async-start(bf16[2,16,4,2048]{3,2,0,1:T(4,128)(2,1)} %copy.72), calls=%async_computation | async-start | bytes 1048576 | tf_op jit(solution)/shard_map/all_to_all | solution.py:113
  40.0 11.8 %copy-start.5 = (bf16[64,128]{1,0:T(8,128)(2,1)S(1)}, bf16[64,128]{1,0:T(8,128)(2,1)}, u32[]{:S(2)}) copy-start(bf16[64,128]{1,0:T(8,128)(2,1)} %param.15) | copy-start | bytes 49156
  48.3 27.2 %all-to-all-start.1 = ((f32[16,1,128]{2,1,0:T(1,128)}), f32[16,1,128]{2,1,0:T(1,128)S(1)}, u32[]{:S(2)}, u32[]{:S(2)}) async-start(f32[16,1,128]{2,1,0:T(1,128)} %reshape.490), calls=%async_computation.1 | async-start | bytes 16384 | tf_op jit(solution)/shard_map/all_to_all | solution.py:121
  75.5 18.0 %all-to-all-start.2 = ((bf16[2,16,4,2048]{3,2,0,1:T(4,128)(2,1)}), bf16[2,16,4,2048]{3,2,0,1:T(4,128)(2,1)S(1)}, u32[]{:S(2)}, u32[]{:S(2)}) async-start(bf16[2,16,4,2048]{3,2,0,1:T(4,128)(2,1)} %copy.79), calls=%async_computation.2 | async-start | bytes 1048576 | tf_op jit(solution)/shard_map/all_to_all | solution.py:118
where the time goes:
time: 96.7 us; the launch traced here: 96.3 us
  blocking collectives  46.6 us (48%)
  starting transfers between devices  14.4 us (15%)
  waiting for transfers between devices  12.3 us (13%)
  local copies, waits for them, and re-layouts  11.6 us (12%)
  other arithmetic  5.59 us (6%)
  matrix products  5.26 us (5%)
    all_gather x1, blocking collectives, body(): key_piece = lax.all_gather(fresh_keys, 'cache', axis=0, tiled=True)  24.2 us
    all_gather x1, blocking collectives, body(): value_piece = lax.all_gather(fresh_values, 'cache', axis=0, tiled=True)  22.4 us
    all_to_all x1, waiting for transfers between devices, body(): lax.all_to_all(partial_out.astype(jnp.float32), 'cache', split_axis=1, co...  12.3 us
    all_to_all x1, starting transfers between devices, body(): lax.all_to_all(outgoing, 'cache', split_axis=1, concat_axis=1, tiled=True)  7.38 us
    all_to_all x1, starting transfers between devices, body(): lax.all_to_all(partial_out.astype(jnp.float32), 'cache', split_axis=1, co...  3.57 us
    all_to_all x1, starting transfers between devices, body(): lax.all_to_all(partial_lse, 'cache', split_axis=1, concat_axis=1, tiled=T...  3.47 us
    reduce_sum x2, other arithmetic, owner_block(): totals = jnp.maximum(jnp.sum(weights, axis=2), 1.0)  2.34 us
    dot_general x2, matrix products, owner_block(): jnp.einsum('thk,kd->thd', weights.astype(jnp.bfloat16), page_values, pref...  2.27 us
  transfers between devices with their start and end apart: 3, of which 1 were waited for; matrix products, arithmetic and copies ran while one was open for 7% of the time, Pallas kernels for 0%

commit v1 on v0

--- a/solution.py
+++ b/solution.py
@@ -3,6 +3,7 @@
 import jax.numpy as jnp
 from jax import lax
 from jax.sharding import PartitionSpec as P
+from jax.lax import all_to_all, axis_size
 
 HEADS = 16
 HD = 128
@@ -115,8 +116,14 @@
         arrived_queries, region_keys, region_values, slot_visible, devices
     )
     returned_out, returned_lse = (
-        lax.all_to_all(
-            partial_out.astype(jnp.float32), "cache", split_axis=1, concat_axis=1, tiled=True
+        jnp.concatenate(
+            all_to_all(
+                jnp.stack(jnp.split(partial_out.astype(jnp.float32), axis_size("cache"), axis=1)),
+                "cache",
+                0,
+                0,
+            ),
+            axis=1,
         ).astype(partial_out.dtype),
         lax.all_to_all(partial_lse, "cache", split_axis=1, concat_axis=1, tiled=True),
     )

time: 96.7 us -> 105 us (1.086)
  other arithmetic: 5.59 us -> 9.79 us
  local copies, waits for them, and re-layouts: 11.6 us -> 15.5 us
  blocking collectives: 46.6 us -> 43.8 us
  starting transfers between devices: 14.4 us -> 16.8 us
    unnamed x0 -> x1, other arithmetic: none -> 4.2 us
    unnamed x23 -> x39, local copies, waits for them, and re-layouts: 1.85 us -> 5.45 us
    all_gather x1, blocking collectives: 22.4 us -> 19.7 us  [body(): value_piece = lax.all_gather(fresh_values, 'cache', axis=0, tiled=True)]
    all_to_all x1, starting transfers between devices: 3.57 us -> 5.79 us  [body(): all_to_all(jnp.stack(jnp.split(partial_out.astype(jnp.float32), axis_size...]
  transfers between devices with their start and end apart: 3 -> 3, of which waited for: 1 -> 1; matrix products, arithmetic and copies ran while one was open for 7% -> 11% of each run, Pallas kernels for 0% -> 0%
where the time goes in v1:
time: 105 us; the launch traced here: 104 us
  blocking collectives  43.8 us (42%)
  starting transfers between devices  16.8 us (16%)
  local copies, waits for them, and re-layouts  15.5 us (15%)
  waiting for transfers between devices  12.3 us (12%)
  other arithmetic  9.79 us (9%)
  matrix products  5.26 us (5%)
    all_gather x1, blocking collectives, body(): key_piece = lax.all_gather(fresh_keys, 'cache', axis=0, tiled=True)  24.2 us
    all_gather x1, blocking collectives, body(): value_piece = lax.all_gather(fresh_values, 'cache', axis=0, tiled=True)  19.7 us
    all_to_all x1, waiting for transfers between devices, body(): all_to_all(jnp.stack(jnp.split(partial_out.astype(jnp.float32), axis_size...  12.3 us
    all_to_all x1, starting transfers between devices, body(): lax.all_to_all(outgoing, 'cache', split_axis=1, concat_axis=1, tiled=True)  7.4 us
    all_to_all x1, starting transfers between devices, body(): all_to_all(jnp.stack(jnp.split(partial_out.astype(jnp.float32), axis_size...  5.79 us
    unnamed x39, local copies, waits for them, and re-layouts  5.45 us
    unnamed x1, other arithmetic  4.2 us
    all_to_all x1, starting transfers between devices, body(): lax.all_to_all(partial_lse, 'cache', split_axis=1, concat_axis=1, tiled=T...  3.65 us
  transfers between devices with their start and end apart: 3, of which 1 were waited for; matrix products, arithmetic and copies ran while one was open for 11% of the time, Pallas kernels for 0%

profile of v1, /device:TPU:0, one launch (start us, length us, event | category | flops | bytes accessed | tf_op | source)
XLA Modules:
  0.0 104.1 jit_solution(12162634488042017397)
XLA Ops:
  0.0 0.8 broadcast_compare_fusion.1
  1.1 1.1 %reshape.333 = bf16[16,4,2048]{2,1,0:T(4,128)(2,1)S(1)} reshape(bf16[64,2048]{1,0:T(8,128)(2,1)} %param.13) | data formatting | bytes 524288 | tf_op jit(solution)/shard_map/reshape | solution.py:112
  2.1 1.0 gather_fusion.1
  3.6 1.2 %copy.160 = bf16[2,16,4,2048]{3,2,0,1:T(4,128)(2,1)} copy(bf16[2,16,4,2048]{3,1,0,2:T(8,128)(2,1)S(1)} %broadcast_select_fusion) | data formatting | bytes 1048576 | tf_op jit(solution)/shard_map/jit(_take)/select_n | solution.py:113
  4.8 7.4 %all-to-all-start = ((bf16[2,16,4,2048]{3,2,0,1:T(4,128)(2,1)}), bf16[2,16,4,2048]{3,2,0,1:T(4,128)(2,1)S(1)}, u32[]{:S(2)}, u32[]{:S(2)}) async-start(bf16[2,16,4,2048]{3,2,0,1:T(4,128)(2,1)} %copy.160), calls=%async_computation | async-start | bytes 1048576 | tf_op jit(solution)/shard_map/all_to_all | solution.py:114
  12.8 0.7 gather_fusion.4
  13.9 24.2 %all_gather.6 = bf16[1024,128]{1,0:T(8,128)(2,1)S(1)} all-gather(bf16[64,128]{1,0:T(8,128)(2,1)S(1)} %copy-done.4), channel_id=1, replica_groups=mesh['groups'=2,'cache'=16] {'cache'}, dimensions={0}, use_global_device_ids=true | all-gather | bytes 278528 | tf_op jit(solution)/shard_map/all_gather | solution.py:86
  38.3 19.7 %all_gather.7 = bf16[1024,128]{1,0:T(8,128)(2,1)S(1)} all-gather(bf16[64,128]{1,0:T(8,128)(2,1)S(1)} %copy-done.5), channel_id=1, replica_groups=mesh['groups'=2,'cache'=16] {'cache'}, dimensions={0}, use_global_device_ids=true | all-gather | bytes 278528 | tf_op jit(solution)/shard_map/all_gather | solution.py:87
  58.1 0.6 gather_fusion
  59.8 7.6 %while.20 = (s32[]{:T(128)}, bf16[2,16,4,2048]{3,1,2,0:T(8,128)(2,1)S(1)}, f32[2,16,4,16]{3,2,0,1:T(4,128)S(1)}, pred[2,1024]{1,0:T(4,128)(4,1)S(1)}, bf16[2,16,...) while((s32[]{:T(128)}, ...), condition=%wide.region_8.9_spmd, body=%wide.region_5.0_spmd.sunk | while | flops 550765568 | bytes 18004104 | solution.py:51
  60.1 0.8 fusion.73
  61.0 1.2 %fusion.74 = f32[64,16]{1,0:T(8,128)S(1)} fusion(f32[64,16,1024]{2,1,0:T(8,128)S(1)} %get-tuple-element.216, f32[1024]{0:T(1024)S(1)} %convert_element_type.86, f32[64,16]{1,0:T(8,128)S(1)} %get-tuple-element.217, pred[1024]{0:T(1024)(128)(4,1)S(1)} %dynamic-slice_reduce_fusion.2), kind=kLoop, calls=%fused_computation.8.clone.1 | loop fusion | flops 5241856 | bytes 4207616 | tf_op jit(solution)/shard_map/while/body/eval_jaxpr/while/body/eval_jaxpr/reduce_sum | solution.py:27
  62.2 1.1 %fusion.75 = bf16[64,16,128]{2,1,0:T(8,128)(2,1)S(1)} fusion(f32[64,16,1024]{2,1,0:T(8,128)S(1)} %get-tuple-element.216, f32[1024]{0:T(1024)S(1)} %convert_element_type.86, f32[64,16]{1,0:T(8,128)S(1)} %get-tuple-element.217, pred[1024]{0:T(1024)(128)(4,1)S(1)} %dynamic-slice_reduce_fusion.2, f32[64,16]{1,0:T(8,128)S(1)} %get-tuple-element.218, ...), kind=kOutput, calls=%fused_computation.13.clone.1 | convolution fusion | flops 273940480 | bytes 4789252 | tf_op jit(solution)/shard_map/while/body/eval_jaxpr/while/body/eval_jaxpr/thk,kd->thd/dot_general | solution.py:28
  63.9 0.8 fusion.73
  64.8 1.2 %fusion.74 = f32[64,16]{1,0:T(8,128)S(1)} fusion(f32[64,16,1024]{2,1,0:T(8,128)S(1)} %get-tuple-element.216, f32[1024]{0:T(1024)S(1)} %convert_element_type.86, f32[64,16]{1,0:T(8,128)S(1)} %get-tuple-element.217, pred[1024]{0:T(1024)(128)(4,1)S(1)} %dynamic-slice_reduce_fusion.2), kind=kLoop, calls=%fused_computation.8.clone.1 | loop fusion | flops 5241856 | bytes 4207616 | tf_op jit(solution)/shard_map/while/body/eval_jaxpr/while/body/eval_jaxpr/reduce_sum | solution.py:27
  66.0 1.1 %fusion.75 = bf16[64,16,128]{2,1,0:T(8,128)(2,1)S(1)} fusion(f32[64,16,1024]{2,1,0:T(8,128)S(1)} %get-tuple-element.216, f32[1024]{0:T(1024)S(1)} %convert_element_type.86, f32[64,16]{1,0:T(8,128)S(1)} %get-tuple-element.217, pred[1024]{0:T(1024)(128)(4,1)S(1)} %dynamic-slice_reduce_fusion.2, f32[64,16]{1,0:T(8,128)S(1)} %get-tuple-element.218, ...), kind=kOutput, calls=%fused_computation.13.clone.1 | convolution fusion | flops 273940480 | bytes 4789252 | tf_op jit(solution)/shard_map/while/body/eval_jaxpr/while/body/eval_jaxpr/thk,kd->thd/dot_general | solution.py:28
  68.6 0.7 reshape.491
  69.3 3.7 %all-to-all-start.1 = ((f32[16,1,128]{2,1,0:T(1,128)}), f32[16,1,128]{2,1,0:T(1,128)S(1)}, u32[]{:S(2)}, u32[]{:S(2)}) async-start(f32[16,1,128]{2,1,0:T(1,128)} %reshape.491), calls=%async_computation.1 | async-start | bytes 16384 | tf_op jit(solution)/shard_map/all_to_all | solution.py:128
  73.1 0.6 broadcast.507
  73.7 4.2 %reduce.11 = bf16[16,2,4,2048]{3,2,1,0:T(4,128)(2,1)S(1)} reduce(bf16[16,2,4,1,2048]{4,3,2,1,0:T(2,128)(2,1)S(1)} %bitcast.171, bf16[]{:T(256)} %broadcast.507), dimensions={3}, to_apply=%bitcast.145.reduce_sub_computation | reduce | bytes 1048578
  77.9 1.3 %reshape.493 = bf16[16,2,8192]{2,1,0:T(2,128)(2,1)} reshape(bf16[16,2,4,2048]{3,2,1,0:T(4,128)(2,1)S(1)} %reduce.11) | data formatting | bytes 1048576
  79.2 5.8 %all-to-all-start.2 = ((bf16[16,2,8192]{2,1,0:T(2,128)(2,1)}), bf16[16,2,8192]{2,1,0:T(2,128)(2,1)S(1)}, u32[]{:S(2)}, u32[]{:S(2)}) async-start(bf16[16,2,8192]{2,1,0:T(2,128)(2,1)} %reshape.493), calls=%async_computation.2 | async-start | bytes 1048576 | tf_op jit(solution)/shard_map/all_to_all | solution.py:120
  85.0 0.5 broadcast.506
  85.5 0.7 reduce.10
  86.3 0.6 gather_fusion.2
  87.2 12.3 %all-to-all-done.2 = bf16[16,2,8192]{2,1,0:T(2,128)(2,1)S(1)} async-done(((bf16[16,2,8192]{2,1,0:T(2,128)(2,1)}), bf16[16,2,8192]{2,1,0:T(2,128)(2,1)S(1)}, u32[]{:S(2)}, u32[]{:S(2)}) %all-to-all-start.2) | async-done | bytes 524320 | tf_op jit(solution)/shard_map/all_to_all | solution.py:120
  99.5 0.5 reshape.494
  100.0 1.1 %bitcast_bitcast_fusion = bf16[2,16,1,4,2048]{4,2,3,0,1:T(2,128)(2,1)S(1)} fusion(bf16[16,2,4,1,2048]{4,3,2,1,0:T(2,128)(2,1)S(1)} %reshape.494), kind=kLoop, calls=%fused_computation.126 | loop fusion | bytes 1048576 | tf_op jit(solution)/shard_map/convert_element_type | solution.py:127
  101.1 0.6 copy.167
  101.8 0.6 gather_fusion.3
  102.4 1.0 fusion.25
  103.4 0.8 copy.185
  (99 shorter events, 5.8 us)
Async XLA Ops:
  0.0 58.1 %copy-start = (s32[16]{0:T(128)S(1)}, s32[16]{0:T(128)}, u32[]{:S(2)}) copy-start(s32[16]{0:T(128)} %param.10) | copy-start | bytes 196
  0.0 12.2 %copy-start.6 = (s32[16,1]{0,1:T(1,128)S(1)}, s32[16,1]{0,1:T(1,128)}, u32[]{:S(2)}) copy-start(s32[16,1]{0,1:T(1,128)} %param.11) | copy-start | bytes 196
  0.0 38.2 %copy-start.2 = (bf16[64,2048]{1,0:T(8,128)(2,1)S(1)}, bf16[64,2048]{1,0:T(8,128)(2,1)}, u32[]{:S(2)}) copy-start(bf16[64,2048]{1,0:T(8,128)(2,1)} %param.13) | copy-start | bytes 786436
  0.0 12.2 %copy-start.3 = (s32[16,16]{1,0:T(8,128)S(1)}, s32[16,16]{1,0:T(8,128)}, u32[]{:S(2)}) copy-start(s32[16,16]{1,0:T(8,128)} %param.12) | copy-start | bytes 3076
  0.0 13.9 %copy-start.4 = (bf16[64,128]{1,0:T(8,128)(2,1)S(1)}, bf16[64,128]{1,0:T(8,128)(2,1)}, u32[]{:S(2)}) copy-start(bf16[64,128]{1,0:T(8,128)(2,1)} %param.14) | copy-start | bytes 49156
  0.0 38.3 %copy-start.5 = (bf16[64,128]{1,0:T(8,128)(2,1)S(1)}, bf16[64,128]{1,0:T(8,128)(2,1)}, u32[]{:S(2)}) copy-start(bf16[64,128]{1,0:T(8,128)(2,1)} %param.15) | copy-start | bytes 49156
  3.4 56.3 %copy-start.1 = (bf16[2048,128]{1,0:T(8,128)(2,1)S(1)}, bf16[2048,128]{1,0:T(8,128)(2,1)}, u32[]{:S(2)}) copy-start(bf16[2048,128]{1,0:T(8,128)(2,1)} %param.16) | copy-start | bytes 1572868
  4.8 55.0 %all-to-all-start = ((bf16[2,16,4,2048]{3,2,0,1:T(4,128)(2,1)}), bf16[2,16,4,2048]{3,2,0,1:T(4,128)(2,1)S(1)}, u32[]{:S(2)}, u32[]{:S(2)}) async-start(bf16[2,16,4,2048]{3,2,0,1:T(4,128)(2,1)} %copy.160), calls=%async_computation | async-start | bytes 1048576 | tf_op jit(solution)/shard_map/all_to_all | solution.py:114
  60.1 2.1 %copy-start.7 = (bf16[2,1024,128]{2,1,0:T(8,128)(2,1)S(1)}, bf16[2,1024,128]{2,1,0:T(8,128)(2,1)}, u32[]{:S(2)}) copy-start(bf16[2,1024,128]{2,1,0:T(8,128)(2,1)} %get-tuple-element.242) | copy-start | bytes 1572868 | tf_op jit(solution)/shard_map/while
  63.9 2.1 %copy-start.7 = (bf16[2,1024,128]{2,1,0:T(8,128)(2,1)S(1)}, bf16[2,1024,128]{2,1,0:T(8,128)(2,1)}, u32[]{:S(2)}) copy-start(bf16[2,1024,128]{2,1,0:T(8,128)(2,1)} %get-tuple-element.242) | copy-start | bytes 1572868 | tf_op jit(solution)/shard_map/while
  69.3 9.9 %all-to-all-start.1 = ((f32[16,1,128]{2,1,0:T(1,128)}), f32[16,1,128]{2,1,0:T(1,128)S(1)}, u32[]{:S(2)}, u32[]{:S(2)}) async-start(f32[16,1,128]{2,1,0:T(1,128)} %reshape.491), calls=%async_computation.1 | async-start | bytes 16384 | tf_op jit(solution)/shard_map/all_to_all | solution.py:128
  79.2 20.3 %all-to-all-start.2 = ((bf16[16,2,8192]{2,1,0:T(2,128)(2,1)}), bf16[16,2,8192]{2,1,0:T(2,128)(2,1)S(1)}, u32[]{:S(2)}, u32[]{:S(2)}) async-start(bf16[16,2,8192]{2,1,0:T(2,128)(2,1)} %reshape.493), calls=%async_computation.2 | async-start | bytes 1048576 | tf_op jit(solution)/shard_map/all_to_all | solution.py:120
